TPU v7x, 32 devices: a whole 2x2x4 slice. The times are simulated.
32 devices in a mesh: expert: 8 (over y, x, core), tensor: 4 (over z).
Axes of the slice: x: 2, y: 2, z: 4, core: 2. Of those that a mesh axis runs over, the one named last changes fastest.
Arguments:
- tokens: bfloat16 [4096, 2560], P(('expert', 'tensor')), may hold values from -6 to 6
- expert_ids: int32 [4096, 1], P(('expert', 'tensor')), may hold values from 0 to 7; in each aligned block of 512 rows (0 to 511, 512 to 1023, ...) at most 128 rows name the same one
- gates: float32 [4096], P(('expert', 'tensor')), may hold values from 0.3 to 3
- w_gate: bfloat16 [8, 2560, 4096], P('expert', None, 'tensor'), may hold values from -0.125 to 0.125
- w_up: bfloat16 [8, 2560, 4096], P('expert', None, 'tensor'), may hold values from -0.125 to 0.125
- w_down: bfloat16 [8, 4096, 2560], P('expert', 'tensor'), may hold values from -0.09375 to 0.09375
- s_gate: bfloat16 [2560, 4096], P('expert', 'tensor'), may hold values from -0.125 to 0.125
- s_up: bfloat16 [2560, 4096], P('expert', 'tensor'), may hold values from -0.125 to 0.125
- s_down: bfloat16 [4096, 2560], P('tensor', 'expert'), may hold values from -0.09375 to 0.09375
Outputs:
- mixed: bfloat16 [4096, 2560], P(('expert', 'tensor'))
Inputs may be any that keep to these rules, and one draw needn't show every extreme that they name: `expert_ids`: in each aligned block of 512 tokens no expert is named by more than 128 tokens, and some block has an expert named by exactly 128 tokens.
All inputs are finite; a program needn't handle non-finite values.
Results may differ from a plain program's by a relative error of at most 0.013.
Values may be sent and summed in bfloat16 or wider, within the bound.
No kernel may reach another device: no remote copies, remote signals or barrier semaphores. Data moves between devices by JAX's collectives and lax.ppermute only.
A program may use at most 128 MiB of HBM per device.

v0:
```python
import jax
import jax.numpy as jnp
from jax import lax
from jax.sharding import PartitionSpec as P


def slots_of(ids, experts, cap):
    onehot = (ids[:, None] == jnp.arange(experts, dtype=jnp.int32)[None, :]).astype(jnp.int32)
    before = jnp.cumsum(onehot, axis=0) - onehot
    position = jnp.sum(before * onehot, axis=1)
    return ids * cap + position


def pick_rows(values, index):
    padded = jnp.concatenate([values, jnp.zeros((1, values.shape[1]), values.dtype)], axis=0)
    return jnp.take(padded, index, axis=0)


def body(tokens, expert_ids, gates, w_gate, w_up, w_down, s_gate, s_up, s_down):
    n_expert = lax.axis_size("expert")
    width = tokens.shape[1]
    group = lax.all_gather(tokens, "tensor", axis=0, tiled=True)
    group_ids = lax.all_gather(expert_ids, "tensor", axis=0, tiled=True)[:, 0]
    group_gates = lax.all_gather(gates, "tensor", axis=0, tiled=True)
    count = group.shape[0]
    experts = w_gate.shape[0] * n_expert
    cap = 2 * count // experts
    shared_gate = jnp.dot(
        group,
        lax.all_gather(s_gate, "expert", axis=0, tiled=True),
        preferred_element_type=jnp.float32,
    )
    shared_upper = jnp.dot(
        group,
        lax.all_gather(s_up, "expert", axis=0, tiled=True),
        preferred_element_type=jnp.float32,
    )
    shared_hidden = (jax.nn.silu(shared_gate) * shared_upper).astype(jnp.bfloat16)
    shared_part = jnp.dot(
        shared_hidden,
        lax.all_gather(s_down, "expert", axis=1, tiled=True),
        preferred_element_type=jnp.float32,
    )
    slot = slots_of(group_ids, experts, cap)
    owner = (
        jnp.full((experts * cap,), count, jnp.int32)
        .at[slot]
        .set(jnp.arange(count, dtype=jnp.int32))
    )
    outgoing = pick_rows(group, owner).reshape(experts, cap, width)
    received = lax.all_to_all(outgoing, "expert", split_axis=0, concat_axis=0, tiled=True)
    flat = received.reshape(-1, width)
    gate = jnp.dot(flat, w_gate[0], preferred_element_type=jnp.float32)
    upper = jnp.dot(flat, w_up[0], preferred_element_type=jnp.float32)
    hidden = (jax.nn.silu(gate) * upper).astype(jnp.bfloat16)
    result = jnp.dot(hidden, w_down[0], preferred_element_type=jnp.float32).astype(jnp.bfloat16)
    produced = result.reshape(received.shape[0], -1, width)
    returned = lax.all_to_all(produced, "expert", split_axis=0, concat_axis=0, tiled=True)
    routed_part = pick_rows(returned.reshape(experts * cap, width), slot).astype(jnp.float32)
    combined = (shared_part + group_gates[:, None] * routed_part).astype(jnp.bfloat16)
    return (
        lax.psum_scatter(combined, "tensor", scatter_dimension=0, tiled=True)
        .astype(jnp.float32)
        .astype(jnp.bfloat16)
    )


def solution(mesh):
    return jax.shard_map(
        body,
        mesh=mesh,
        in_specs=(
            P(("expert", "tensor"), None),
            P(("expert", "tensor"), None),
            P(("expert", "tensor")),
            P("expert", None, "tensor"),
            P("expert", None, "tensor"),
            P("expert", "tensor", None),
            P("expert", "tensor"),
            P("expert", "tensor"),
            P("tensor", "expert"),
        ),
        out_specs=P(("expert", "tensor"), None),
        check_vma=False,
    )
```

profile of v0, /device:TPU:0, one launch (start us, length us, event | category | flops | bytes accessed | tf_op | source)
XLA Modules:
  0.0 360.3 jit_solution(4594958189391389571)
XLA Ops:
  6.5 0.0 all-gather.6.cloned.1.call-start
  6.5 0.7 all-gather.6.cloned.1.call-update
  7.3 0.0 all-gather.8.cloned.1.call-start
  7.3 0.7 all-gather.8.cloned.1.call-update
  8.0 0.0 all-gather.10.cloned.1.call-start
  8.1 0.7 all-gather.10.cloned.1.call-update
  8.7 12.8 %all_gather.23 = s32[512,1]{0,1:T(1,128)S(1)} all-gather(s32[128,1]{0,1:T(1,128)} %param.10), channel_id=1, replica_groups=mesh['expert'=8,'tensor'=4] {'tensor'}, dimensions={0}, use_global_device_ids=true | all-gather | bytes 2560 | tf_op jit(solution)/shard_map/all_gather | solution.py:23
  21.5 1.1 reduce-window.6
  22.7 0.2 slice_reduce_fusion
  22.9 0.1 fusion.10
  23.1 2.4 scatter_custom_fusion
  25.5 40.9 %all-gather.6.cloned.1.call-done = bf16[512,2560]{1,0:T(8,128)(2,1)} async-done(((bf16[128,2560]{1,0:T(8,128)(2,1)}), bf16[512,2560]{1,0:T(8,128)(2,1)}) %all-gather.6.cloned.1.call-update) | async-done | bytes 2621456 | tf_op jit(solution)/shard_map/all_gather | solution.py:22
  66.4 1.9 concatenate.6
  68.3 6.4 %gather_fusion = bf16[1024,2560]{1,0:T(8,128)(2,1)} fusion(bf16[513,2560]{1,0:T(8,128)(2,1)S(1)} %concatenate.6, s32[1024]{0:T(1024)S(1)} %fusion.12), kind=kCustom, calls=%fused_computation | custom fusion | bytes 10489856 | tf_op jit(solution)/shard_map/jit(_take)/gather | solution.py:16
  74.7 5.5 %broadcast_select_fusion = bf16[8,128,2560]{2,1,0:T(8,128)(2,1)} fusion(bf16[8,128,2560]{2,1,0:T(8,128)(2,1)} %bitcast.41, pred[8,128]{1,0:T(8,128)(4,1)S(1)} %and_bitcast_fusion), kind=kLoop, calls=%fused_computation.10 | loop fusion | flops 2621440 | bytes 10486784 | tf_op jit(solution)/shard_map/jit(_take)/select_n | solution.py:16
  80.2 4.6 %all-to-all-start = ((bf16[8,128,2560]{2,1,0:T(8,128)(2,1)}), bf16[8,128,2560]{2,1,0:T(8,128)(2,1)}, u32[]{:S(2)}, u32[]{:S(2)}) async-start(bf16[8,128,2560]{2,1,0:T(8,128)(2,1)} %broadcast_select_fusion), calls=%async_computation | async-start | bytes 10485760 | tf_op jit(solution)/shard_map/all_to_all | solution.py:51
  84.8 0.0 all-gather.12.cloned.1.call-start
  84.9 0.5 all-gather.12.cloned.1.call-update
  85.4 80.8 %all-to-all-done = bf16[8,128,2560]{2,1,0:T(8,128)(2,1)} async-done(((bf16[8,128,2560]{2,1,0:T(8,128)(2,1)}), bf16[8,128,2560]{2,1,0:T(8,128)(2,1)}, u32[]{:S(2)}, u32[]{:S(2)}) %all-to-all-start) | async-done | bytes 5242912 | tf_op jit(solution)/shard_map/all_to_all | solution.py:51
  166.2 11.2 %fusion.1 = f32[1024,1024]{1,0:T(8,128)} fusion(bf16[1024,2560]{1,0:T(8,128)(2,1)} %bitcast.10, bf16[1,2560,1024]{2,1,0:T(8,128)(2,1)} %param.13), kind=kOutput, calls=%fused_computation.5 | convolution fusion | flops 5368709120 | bytes 14680064 | tf_op jit(solution)/shard_map/dot_general | solution.py:54
  177.4 18.6 %convolution_convert_fusion = bf16[1024,2560]{1,0:T(8,128)(2,1)} fusion(bf16[1,1024,2560]{2,1,0:T(8,128)(2,1)} %param.14, f32[1024,1024]{1,0:T(8,128)} %fusion.1, bf16[1024,2560]{1,0:T(8,128)(2,1)} %bitcast.10, bf16[1,2560,1024]{2,1,0:T(8,128)(2,1)} %param.12), kind=kOutput, calls=%fused_computation.3 | convolution fusion | flops 10746331136 | bytes 25165824 | tf_op jit(solution)/shard_map/dot_general | solution.py:56
  196.0 0.0 copy-start.1
  196.0 0.0 copy-start
  196.0 4.9 %all-to-all-start.1 = ((bf16[8,128,2560]{2,1,0:T(8,128)(2,1)}), bf16[8,128,2560]{2,1,0:T(8,128)(2,1)}, u32[]{:S(2)}, u32[]{:S(2)}) async-start(bf16[8,128,2560]{2,1,0:T(8,128)(2,1)} %bitcast.42), calls=%async_computation.1 | async-start | bytes 10485760 | tf_op jit(solution)/shard_map/all_to_all | solution.py:58
  200.9 0.0 reduce-scatter.2.cloned.1.call-start
  201.0 0.0 copy-done.1
  201.0 7.8 %all-gather = f32[4,1,128]{2,1,0:T(1,128)S(1)} all-gather(f32[1,1,128]{2,1,0:T(1,128)S(1)} %bitcast.50), channel_id=1, replica_groups=mesh['expert'=8,'tensor'=4] {'tensor'}, dimensions={0}, use_global_device_ids=true | all-gather | bytes 2560 | tf_op jit(solution)/shard_map/all_gather | solution.py:24
  208.8 0.0 all-gather.8.cloned.1.call-done
  208.8 0.0 copy-done
  208.8 6.7 %fusion.17 = f32[512,1024]{1,0:T(8,128)} fusion(bf16[512,2560]{1,0:T(8,128)(2,1)S(1)} %copy-done, bf16[2560,1024]{1,0:T(8,128)(2,1)} %all-gather.8.cloned.1.call-done), kind=kOutput, calls=%fused_computation.32 | convolution fusion | flops 2684354560 | bytes 9961472 | tf_op jit(solution)/shard_map/dot_general | solution.py:28
  215.5 60.2 %all-to-all-done.1 = bf16[8,128,2560]{2,1,0:T(8,128)(2,1)} async-done(((bf16[8,128,2560]{2,1,0:T(8,128)(2,1)}), bf16[8,128,2560]{2,1,0:T(8,128)(2,1)}, u32[]{:S(2)}, u32[]{:S(2)}) %all-to-all-start.1) | async-done | bytes 5242912 | tf_op jit(solution)/shard_map/all_to_all | solution.py:58
  275.7 5.1 %concatenate.7 = bf16[1025,2560]{1,0:T(8,128)(2,1)} pad(bf16[1024,2560]{1,0:T(8,128)(2,1)} %bitcast.15, bf16[]{:T(256)} %constant.45.clone.1), padding=0_1x0_0 | pad | bytes 10490882 | tf_op jit(solution)/shard_map/concatenate | solution.py:15
  280.8 8.4 %gather_fusion.1 = bf16[512,2560]{1,0:T(8,128)(2,1)S(1)} fusion(bf16[1025,2560]{1,0:T(8,128)(2,1)} %concatenate.7, s32[1024]{0:T(1024)S(1)} %pad_clamp_fusion), kind=kCustom, calls=%fused_computation.1 | custom fusion | bytes 5244928 | tf_op jit(solution)/shard_map/jit(_take)/gather | solution.py:16
  289.2 0.0 all-gather.10.cloned.1.call-done
  289.2 0.0 all-gather.12.cloned.1.call-done
  289.3 12.6 %add_convert_fusion = bf16[512,2560]{1,0:T(8,128)(2,1)} fusion(bf16[1024,2560]{0,1:T(8,128)(2,1)} %all-gather.12.cloned.1.call-done, bf16[512,2560]{1,0:T(8,128)(2,1)S(1)} %gather_fusion.1, f32[512]{0:T(512)S(1)} %bitcast.49, pred[512]{0:T(512)(128)(4,1)S(1)} %get-tuple-element.5, f32[512,1024]{1,0:T(8,128)} %fusion.17, ...), kind=kOutput, calls=%fused_computation.9 | convolution fusion | flops 5378408448 | bytes 20449792 | tf_op jit(solution)/shard_map/dot_general | solution.py:39
  301.9 0.0 reduce-scatter.2.cloned.1.call-update
  301.9 51.8 %reduce-scatter.2.cloned.1.call-done = bf16[128,2560]{1,0:T(8,128)(2,1)} async-done(((bf16[512,2560]{1,0:T(8,128)(2,1)}), bf16[128,2560]{1,0:T(8,128)(2,1)}) %reduce-scatter.2.cloned.1.call-update) | async-done | bytes 655376 | tf_op jit(solution)/shard_map/reduce_scatter | solution.py:62
  (9 shorter events, 0.1 us)
Async XLA Ops:
  6.5 59.9 %all-gather.6.cloned.1.call-start = ((), (), s32[]{:S(2)}) async-start(), calls=%async_computation.3 | async-start | bytes 3276800 | tf_op jit(solution)/shard_map/all_gather | solution.py:22
  7.3 201.6 %all-gather.8.cloned.1.call-start = ((), (), s32[]{:S(2)}) async-start(), calls=%async_computation.4 | async-start | bytes 5898240 | tf_op jit(solution)/shard_map/all_gather | solution.py:30
  8.0 281.2 %all-gather.10.cloned.1.call-start = ((), (), s32[]{:S(2)}) async-start(), calls=%async_computation.5 | async-start | bytes 5898240 | tf_op jit(solution)/shard_map/all_gather | solution.py:35
  80.2 86.0 %all-to-all-start = ((bf16[8,128,2560]{2,1,0:T(8,128)(2,1)}), bf16[8,128,2560]{2,1,0:T(8,128)(2,1)}, u32[]{:S(2)}, u32[]{:S(2)}) async-start(bf16[8,128,2560]{2,1,0:T(8,128)(2,1)} %broadcast_select_fusion), calls=%async_computation | async-start | bytes 10485760 | tf_op jit(solution)/shard_map/all_to_all | solution.py:51
  84.8 204.5 %all-gather.12.cloned.1.call-start = ((), (), s32[]{:S(2)}) async-start(), calls=%async_computation.6 | async-start | bytes 5898240 | tf_op jit(solution)/shard_map/all_gather | solution.py:41
  196.0 5.0 %copy-start.1 = (f32[128]{0:T(128)S(1)}, f32[128]{0:T(128)}, u32[]{:S(2)}) copy-start(f32[128]{0:T(128)} %param.11) | copy-start | bytes 1540
  196.0 12.9 %copy-start = (bf16[512,2560]{1,0:T(8,128)(2,1)S(1)}, bf16[512,2560]{1,0:T(8,128)(2,1)}, u32[]{:S(2)}) copy-start(bf16[512,2560]{1,0:T(8,128)(2,1)} %all-gather.6.cloned.1.call-done) | copy-start | bytes 7864324
  196.0 79.7 %all-to-all-start.1 = ((bf16[8,128,2560]{2,1,0:T(8,128)(2,1)}), bf16[8,128,2560]{2,1,0:T(8,128)(2,1)}, u32[]{:S(2)}, u32[]{:S(2)}) async-start(bf16[8,128,2560]{2,1,0:T(8,128)(2,1)} %bitcast.42), calls=%async_computation.1 | async-start | bytes 10485760 | tf_op jit(solution)/shard_map/all_to_all | solution.py:58
  200.9 152.8 %reduce-scatter.2.cloned.1.call-start = ((), (), s32[]{:S(2)}) async-start(), calls=%async_computation.7 | async-start | bytes 3276800 | tf_op jit(solution)/shard_map/reduce_scatter | solution.py:62
Sparse Core Ops, SparseCore 0:
  8.9 57.4 all-gather.5
  68.3 67.9 all-gather.7
  138.1 47.1 all-gather.9
  187.1 75.5 all-gather.11
  302.0 51.6 reduce-scatter.1
where the time goes:
time: 361 us; the launch traced here: 360 us
  waiting for transfers between devices  236 us (65%)
  matrix products  49.1 us (14%)
  local copies, waits for them, and re-layouts  24.5 us (7%)
  blocking collectives  20.6 us (6%)
  between operations  13.3 us (4%)
  starting transfers between devices  9.71 us (3%)
  other arithmetic  6.81 us (2%)
    all_to_all x1, waiting for transfers between devices, body(): lax.all_to_all(outgoing, 'expert', split_axis=0, concat_axis=0, tiled=True)  80.8 us
    all_to_all x1, waiting for transfers between devices, body(): lax.all_to_all(produced, 'expert', split_axis=0, concat_axis=0, tiled=True)  60.2 us
    reduce_scatter x1, waiting for transfers between devices, body(): lax.psum_scatter(combined, 'tensor', scatter_dimension=0, tiled=True)  51.8 us
    all_gather x1, waiting for transfers between devices, body(): group = lax.all_gather(tokens, 'tensor', axis=0, tiled=True)  40.9 us
    dot_general x1, matrix products, body(): jnp.dot(hidden, w_down[0], preferred_element_type=jnp.float32)  18.6 us
    gather x2, local copies, waits for them, and re-layouts, pick_rows(): return jnp.take(padded, index, axis=0)  14.7 us
    all_gather x1, blocking collectives, body(): group_ids = lax.all_gather(expert_ids, 'tensor', axis=0, tiled=True)[:, 0]  12.8 us
    dot_general x1, matrix products, body(): jnp.dot(shared_hidden, lax.all_gather(s_down, 'expert', axis=1, tiled=Tru...  12.6 us
  transfers between devices with their start and end apart: 7, of which 4 were waited for; matrix products, arithmetic and copies ran while one was open for 19% of the time, Pallas kernels for 0%

commit v1 on v0

v1 whole, which is shorter than its diff:
```python
import jax
import jax.numpy as jnp
from jax import lax
from jax.sharding import PartitionSpec as P

CHUNKS = 2
F32 = jnp.float32
BF16 = jnp.bfloat16


def dot(a, b):
    return jnp.dot(a, b, preferred_element_type=F32)


def line_gather(block, count, place):
    up, down, ups, downs = block, block, [], []
    for step in range(1, count):
        up = lax.ppermute(up, "tensor", [(i, i + 1) for i in range(step - 1, count - 1)])
        down = lax.ppermute(down, "tensor", [(i, i - 1) for i in range(1, count - step + 1)])
        ups.append(up)
        downs.append(down)
    parts = [block]
    for back in range(1, count):
        parts.append(jnp.where(place >= back, ups[back - 1], downs[count - back - 1]))
    return jnp.concatenate(parts, axis=0)


def line_scatter(total, count):
    rows = total.shape[0] // count
    part = [total[k * rows:(k + 1) * rows] for k in range(count)]
    up = down = None
    for step in range(1, count):
        first, second = part[step], part[count - step]
        if up is not None:
            first = (first.astype(F32) + up.astype(F32)).astype(BF16)
            second = (second.astype(F32) + down.astype(F32)).astype(BF16)
        up = lax.ppermute(first, "tensor", [(i, i + 1) for i in range(step)])
        down = lax.ppermute(second, "tensor", [(i, i - 1) for i in range(count - step, count)])
    out = part[0].astype(F32)
    if up is not None:
        out = out + up.astype(F32) + down.astype(F32)
    return out.astype(BF16)


def body(tokens, expert_ids, gates, w_gate, w_up, w_down, s_gate, s_up, s_down):
    n_expert = lax.axis_size("expert")
    count = lax.axis_size("tensor")
    place = lax.axis_index("tensor")
    rows, width = tokens.shape
    group = rows * count
    experts = w_gate.shape[0] * n_expert
    cap = 2 * group // experts
    cuts = [width * c // CHUNKS for c in range(CHUNKS + 1)]
    spans = [slice(cuts[c], cuts[c + 1]) for c in range(CHUNKS)]

    inner = s_gate.shape[1]
    s_in = lax.all_gather(jnp.concatenate([s_gate, s_up], axis=1), "expert", axis=0, tiled=True)
    gathered = [line_gather(tokens[:, s], count, place) for s in spans]
    meta = jnp.concatenate([expert_ids.astype(F32).T, gates[None, :]], axis=0)
    meta = lax.all_gather(meta, "tensor", axis=0, tiled=False)[::-1]
    meta = lax.dynamic_slice_in_dim(jnp.concatenate([meta, meta]), count - 1 - place, count)
    ids = meta[:, 0, :].reshape(group).astype(jnp.int32)
    scale = meta[:, 1, :].reshape(group)

    index = jnp.arange(group, dtype=jnp.int32)
    same = (ids[:, None] == ids[None, :]) & (index[None, :] < index[:, None])
    slot = ids * cap + jnp.sum(same.astype(jnp.int32), axis=1)
    places = jnp.arange(experts * cap, dtype=jnp.int32)
    into = (places[:, None] == slot[None, :]).astype(BF16)
    outof = (slot[:, None] == places[None, :]).astype(BF16)

    gate = upper = None
    for s, part in zip(spans, gathered):
        sent = dot(into, part).astype(BF16).reshape(experts, cap, -1)
        got = lax.all_to_all(sent, "expert", split_axis=0, concat_axis=0, tiled=True)
        got = got.reshape(experts * cap, -1)
        g, u = dot(got, w_gate[0, s]), dot(got, w_up[0, s])
        gate, upper = (g, u) if gate is None else (gate + g, upper + u)
    hidden = (jax.nn.silu(gate) * upper).astype(BF16)

    pre = None
    for s, part in zip(spans, gathered):
        term = dot(part, s_in[s])
        pre = term if pre is None else pre + term
    shared = (jax.nn.silu(pre[:, :inner]) * pre[:, inner:]).astype(BF16)
    s_out = lax.all_gather(s_down, "expert", axis=1, tiled=True)

    outs = []
    for s in spans:
        made = dot(hidden, w_down[0, :, s]).astype(BF16).reshape(experts, cap, -1)
        back = lax.all_to_all(made, "expert", split_axis=0, concat_axis=0, tiled=True)
        routed = dot(outof, back.reshape(experts * cap, -1))
        term = (dot(shared, s_out[:, s]) + scale[:, None] * routed).astype(BF16)
        outs.append(line_scatter(term, count))
    return jnp.concatenate(outs, axis=1)


def solution(mesh):
    return jax.shard_map(
        body,
        mesh=mesh,
        in_specs=(
            P(("expert", "tensor"), None),
            P(("expert", "tensor"), None),
            P(("expert", "tensor")),
            P("expert", None, "tensor"),
            P("expert", None, "tensor"),
            P("expert", "tensor", None),
            P("expert", "tensor"),
            P("expert", "tensor"),
            P("tensor", "expert"),
        ),
        out_specs=P(("expert", "tensor"), None),
        check_vma=False,
    )
```

time: 361 us -> 293 us (0.81)
  waiting for transfers between devices: 236 us -> 123 us
  starting transfers between devices: 9.71 us -> 64.7 us
  local copies, waits for them, and re-layouts: 24.5 us -> 2.43 us
  matrix products: 49.1 us -> 66.7 us
  blocking collectives: 20.6 us -> 12.9 us
    all_to_all x2 -> x4, waiting for transfers between devices: 141 us -> 72.9 us  [the longest x2 43.2 us: body(): lax.all_to_all(sent, 'expert', split_axis=0, concat_axis=0, tiled=True)]
    reduce_scatter x1 -> x0, waiting for transfers between devices: 51.8 us -> none  [body(): lax.psum_scatter(combined, 'tensor', scatter_dimension=0, tiled=True)]
    ppermute x0 -> x24, waiting for transfers between devices: none -> 49.8 us  [the longest x6 35.1 us: line_gather(): lax.ppermute(down, 'tensor', [(i, i - 1) for i in range(1, count - step +...]
    ppermute x0 -> x24, starting transfers between devices: none -> 48.1 us  [the longest x6 20.8 us: line_scatter(): up = lax.ppermute(first, 'tensor', [(i, i + 1) for i in range(step)])]
    all_gather x4 -> x2, waiting for transfers between devices: 40.9 us -> 0.02 us  [the longest x1 0.02 us: body(): s_out = lax.all_gather(s_down, 'expert', axis=1, tiled=True)]
    dot_general x4 -> x14, matrix products: 49.1 us -> 66.7 us  [dot(): return jnp.dot(a, b, preferred_element_type=F32)]
    gather x2 -> x0, local copies, waits for them, and re-layouts: 14.7 us -> none  [pick_rows(): return jnp.take(padded, index, axis=0)]
    all_gather x2 -> x1, blocking collectives: 20.6 us -> 12.9 us  [body(): meta = lax.all_gather(meta, 'tensor', axis=0, tiled=False)[::-1]]
  transfers between devices with their start and end apart: 7 -> 30, of which waited for: 4 -> 14; matrix products, arithmetic and copies ran while one was open for 19% -> 24% of each run, Pallas kernels for 0% -> 0%
where the time goes in v1:
time: 293 us; the launch traced here: 292 us
  waiting for transfers between devices  123 us (42%)
  matrix products  66.7 us (23%)
  starting transfers between devices  64.7 us (22%)
  between operations  14.1 us (5%)
  blocking collectives  12.9 us (4%)
  other arithmetic  7.51 us (3%)
    dot_general x14, matrix products, dot(): return jnp.dot(a, b, preferred_element_type=F32)  66.7 us
    all_to_all x2, waiting for transfers between devices, body(): lax.all_to_all(sent, 'expert', split_axis=0, concat_axis=0, tiled=True)  43.2 us
    ppermute x6, waiting for transfers between devices, line_gather(): lax.ppermute(down, 'tensor', [(i, i - 1) for i in range(1, count - step +...  35.1 us
    all_to_all x2, waiting for transfers between devices, body(): lax.all_to_all(made, 'expert', split_axis=0, concat_axis=0, tiled=True)  29.7 us
    ppermute x6, starting transfers between devices, line_scatter(): up = lax.ppermute(first, 'tensor', [(i, i + 1) for i in range(step)])  20.8 us
    ppermute x6, starting transfers between devices, line_gather(): lax.ppermute(up, 'tensor', [(i, i + 1) for i in range(step - 1, count - 1)])  13.6 us
    all_gather x1, blocking collectives, body(): meta = lax.all_gather(meta, 'tensor', axis=0, tiled=False)[::-1]  12.9 us
    ppermute x6, waiting for transfers between devices, line_scatter(): up = lax.ppermute(first, 'tensor', [(i, i + 1) for i in range(step)])  8.38 us
  transfers between devices with their start and end apart: 30, of which 14 were waited for; matrix products, arithmetic and copies ran while one was open for 24% of the time, Pallas kernels for 0%

profile of v1, /device:TPU:0, one launch (start us, length us, event | category | flops | bytes accessed | tf_op | source)
XLA Modules:
  0.0 291.6 jit_solution(7226953212598344813)
XLA Ops:
  6.5 2.5 pad_maximum_fusion.1
  9.2 5.0 %collective-permute-start.6 = (bf16[128,1280]{1,0:T(8,128)(2,1)S(1)}, bf16[128,1280]{1,0:T(8,128)(2,1)S(1)}, u32[]{:S(2)}, u32[]{:S(2)}) collective-permute-start(bf16[128,1280]{1,0:T(8,128)(2,1)S(1)} %get-tuple-element.18), channel_id=1, source_target_pairs={{0,1},{1,2},{2,3},{4,5},{5,6},{6,7},{8,9},{9,10},{10,11},{12,13},{... | collective-permute-start | bytes 983048 | tf_op jit(solution)/shard_map/ppermute | solution.py:18
  14.2 1.3 collective-permute-start.7
  15.5 1.3 collective-permute-start.1
  16.8 5.9 %collective-permute-start = (bf16[128,1280]{1,0:T(8,128)(2,1)S(1)}, bf16[128,1280]{1,0:T(8,128)(2,1)}, u32[]{:S(2)}, u32[]{:S(2)}) collective-permute-start(bf16[128,1280]{1,0:T(8,128)(2,1)S(1)} %get-tuple-element.17), channel_id=1, source_target_pairs={{0,1},{1,2},{2,3},{4,5},{5,6},{6,7},{8,9},{9,10},{10,11},{12,13},{... | collective-permute-start | bytes 983048 | tf_op jit(solution)/shard_map/ppermute | solution.py:18
  22.7 12.9 %all-gather.1 = f32[4,2,128]{2,1,0:T(2,128)S(1)} all-gather(f32[1,2,128]{2,1,0:T(2,128)S(1)} %maximum_bitcast_fusion), channel_id=2, replica_groups=mesh['expert'=8,'tensor'=4] {'tensor'}, dimensions={0}, use_global_device_ids=true | all-gather | bytes 5120 | tf_op jit(solution)/shard_map/all_gather | solution.py:60
  36.3 1.3 collective-permute-start.8
  38.6 8.6 %collective-permute-done.8 = bf16[128,1280]{1,0:T(8,128)(2,1)S(1)} collective-permute-done((bf16[128,1280]{1,0:T(8,128)(2,1)S(1)}, bf16[128,1280]{1,0:T(8,128)(2,1)S(1)}, u32[]{:S(2)}, u32[]{:S(2)}) %collective-permute-start.8) | collective-permute-done | bytes 327712 | tf_op jit(solution)/shard_map/ppermute | solution.py:19
  48.6 7.5 %collective-permute-done.9 = bf16[128,1280]{1,0:T(8,128)(2,1)S(1)} collective-permute-done((bf16[128,1280]{1,0:T(8,128)(2,1)S(1)}, bf16[128,1280]{1,0:T(8,128)(2,1)S(1)}, u32[]{:S(2)}, u32[]{:S(2)}) %collective-permute-start.9) | collective-permute-done | bytes 327712 | tf_op jit(solution)/shard_map/ppermute | solution.py:19
  56.2 3.2 %convolution_convert_fusion = bf16[1024,1280]{1,0:T(8,128)(2,1)} fusion(s32[512]{0:T(512)S(1)} %multiply_add_fusion, bf16[128,1280]{1,0:T(8,128)(2,1)S(1)} %broadcast_select_fusion, bf16[128,1280]{1,0:T(8,128)(2,1)S(1)} %broadcast_select_fusion.2, bf16[128,1280]{1,0:T(8,128)(2,1)S(1)} %broadcast_select_fusion.4, bf16[128,1280]{1,0:T(8,128)(2,1)S(1)} %get-tuple-element.18), kind=kOutput, calls=%fused_computation.5 | convolution fusion | flops 1349255168 | bytes 3934208 | tf_op jit(solution)/shard_map/dot_general | solution.py:12
  59.4 3.7 %all-to-all-start.1 = ((bf16[8,128,1280]{2,1,0:T(8,128)(2,1)}), bf16[8,128,1280]{2,1,0:T(8,128)(2,1)S(1)}, u32[]{:S(2)}, u32[]{:S(2)}) async-start(bf16[8,128,1280]{2,1,0:T(8,128)(2,1)} %bitcast.47), calls=%async_computation.1 | async-start | bytes 5242880 | tf_op jit(solution)/shard_map/all_to_all | solution.py:75
  63.9 1.3 collective-permute-start.2
  65.9 10.2 %collective-permute-done.2 = bf16[128,1280]{1,0:T(8,128)(2,1)S(1)} collective-permute-done((bf16[128,1280]{1,0:T(8,128)(2,1)}, bf16[128,1280]{1,0:T(8,128)(2,1)S(1)}, u32[]{:S(2)}, u32[]{:S(2)}) %collective-permute-start.2) | collective-permute-done | bytes 327712 | tf_op jit(solution)/shard_map/ppermute | solution.py:19
  78.6 8.7 %collective-permute-done.3 = bf16[128,1280]{1,0:T(8,128)(2,1)S(1)} collective-permute-done((bf16[128,1280]{1,0:T(8,128)(2,1)S(1)}, bf16[128,1280]{1,0:T(8,128)(2,1)S(1)}, u32[]{:S(2)}, u32[]{:S(2)}) %collective-permute-start.3) | collective-permute-done | bytes 327712 | tf_op jit(solution)/shard_map/ppermute | solution.py:19
  88.1 3.1 %convolution_convert_fusion.1 = bf16[1024,1280]{1,0:T(8,128)(2,1)} fusion(s32[512]{0:T(512)S(1)} %multiply_add_fusion, bf16[128,1280]{1,0:T(8,128)(2,1)S(1)} %broadcast_select_fusion.1, bf16[128,1280]{1,0:T(8,128)(2,1)S(1)} %broadcast_select_fusion.3, bf16[128,1280]{1,0:T(8,128)(2,1)S(1)} %broadcast_select_fusion.5, bf16[128,1280]{1,0:T(8,128)(2,1)S(1)} %get-tuple-element.17), kind=kOutput, calls=%fused_computation.6 | convolution fusion | flops 1349255168 | bytes 3934208 | tf_op jit(solution)/shard_map/dot_general | solution.py:12
  91.2 10.8 %all-to-all-done.1 = bf16[8,128,1280]{2,1,0:T(8,128)(2,1)S(1)} async-done(((bf16[8,128,1280]{2,1,0:T(8,128)(2,1)}), bf16[8,128,1280]{2,1,0:T(8,128)(2,1)S(1)}, u32[]{:S(2)}, u32[]{:S(2)}) %all-to-all-start.1) | async-done | bytes 2621472 | tf_op jit(solution)/shard_map/all_to_all | solution.py:75
  102.1 4.4 %all-to-all-start = ((bf16[8,128,1280]{2,1,0:T(8,128)(2,1)}), bf16[8,128,1280]{2,1,0:T(8,128)(2,1)}, u32[]{:S(2)}, u32[]{:S(2)}) async-start(bf16[8,128,1280]{2,1,0:T(8,128)(2,1)} %bitcast.49), calls=%async_computation | async-start | bytes 5242880 | tf_op jit(solution)/shard_map/all_to_all | solution.py:75
  107.2 6.1 %fusion.17 = f32[1024,1024]{1,0:T(8,128)} fusion(bf16[1024,1280]{1,0:T(8,128)(2,1)S(1)} %bitcast.45, bf16[1,2560,1024]{2,1,0:T(8,128)(2,1)} %param.13), kind=kOutput, calls=%fused_computation.22 | convolution fusion | flops 2684354560 | bytes 9437184 | tf_op jit(solution)/shard_map/dot_general | solution.py:12
  113.3 32.4 %all-to-all-done = bf16[8,128,1280]{2,1,0:T(8,128)(2,1)} async-done(((bf16[8,128,1280]{2,1,0:T(8,128)(2,1)}), bf16[8,128,1280]{2,1,0:T(8,128)(2,1)}, u32[]{:S(2)}, u32[]{:S(2)}) %all-to-all-start) | async-done | bytes 2621472 | tf_op jit(solution)/shard_map/all_to_all | solution.py:75
  145.7 6.0 %fusion.19 = f32[1024,1024]{1,0:T(8,128)S(1)} fusion(bf16[1024,1280]{1,0:T(8,128)(2,1)} %bitcast.6, bf16[1,2560,1024]{2,1,0:T(8,128)(2,1)} %param.13), kind=kOutput, calls=%fused_computation.24 | convolution fusion | flops 2684354560 | bytes 9437184 | tf_op jit(solution)/shard_map/dot_general | solution.py:12
  151.8 4.8 %fusion.21 = f32[1024,1024]{1,0:T(8,128)S(1)} fusion(bf16[1024,1280]{1,0:T(8,128)(2,1)S(1)} %bitcast.46, bf16[1,2560,1024]{2,1,0:T(8,128)(2,1)} %param.12), kind=kOutput, calls=%fused_computation.26 | convolution fusion | flops 2684354560 | bytes 9437184 | tf_op jit(solution)/shard_map/dot_general | solution.py:12
  156.6 5.7 %multiply_convert_fusion = bf16[1024,1024]{1,0:T(8,128)(2,1)S(1)} fusion(f32[1024,1024]{1,0:T(8,128)S(1)} %fusion.19, f32[1024,1024]{1,0:T(8,128)S(1)} %copy-done.12, f32[1024,1024]{1,0:T(8,128)S(1)} %fusion.21, bf16[1024,1280]{1,0:T(8,128)(2,1)} %bitcast.6, bf16[1,2560,1024]{2,1,0:T(8,128)(2,1)S(1)} %bitcast.57), kind=kOutput, calls=%fused_computation.4 | convolution fusion | flops 2692743168 | bytes 19922944 | tf_op jit(solution)/shard_map/dot_general | solution.py:12
  162.4 4.2 %convolution_convert_fusion.3 = bf16[1024,1280]{1,0:T(8,128)(2,1)} fusion(bf16[1024,1024]{1,0:T(8,128)(2,1)S(1)} %multiply_convert_fusion, bf16[1,1024,2560]{2,1,0:T(8,128)(2,1)S(1)} %bitcast.59), kind=kOutput, calls=%fused_computation.8 | convolution fusion | flops 2685665280 | bytes 7340032 | tf_op jit(solution)/shard_map/dot_general | solution.py:12
  166.6 3.6 %all-to-all-start.2 = ((bf16[8,128,1280]{2,1,0:T(8,128)(2,1)}), bf16[8,128,1280]{2,1,0:T(8,128)(2,1)S(1)}, u32[]{:S(2)}, u32[]{:S(2)}) async-start(bf16[8,128,1280]{2,1,0:T(8,128)(2,1)} %bitcast.50), calls=%async_computation.2 | async-start | bytes 5242880 | tf_op jit(solution)/shard_map/all_to_all | solution.py:91
  170.2 6.8 %convolution_convert_fusion.2 = bf16[1024,1280]{1,0:T(8,128)(2,1)} fusion(bf16[1024,1024]{1,0:T(8,128)(2,1)} %copy-done.13, bf16[1,1024,2560]{2,1,0:T(8,128)(2,1)} %param.14), kind=kOutput, calls=%fused_computation.7 | convolution fusion | flops 2685665280 | bytes 7340032 | tf_op jit(solution)/shard_map/dot_general | solution.py:12
  177.0 7.6 %fusion = f32[512,2048]{1,0:T(8,128)} fusion(bf16[2560,2048]{1,0:T(8,128)(2,1)} %all-gather.5.cloned.1.call-done, bf16[128,1280]{1,0:T(8,128)(2,1)} %copy-done.4, bf16[128,1280]{1,0:T(8,128)(2,1)} %copy-done.3, bf16[128,1280]{1,0:T(8,128)(2,1)} %copy-done.5, bf16[128,1280]{1,0:T(8,128)(2,1)S(1)} %get-tuple-element.18), kind=kOutput, calls=%fused_computation | convolution fusion | flops 2689597440 | bytes 10747904 | tf_op jit(solution)/shard_map/dot_general | solution.py:12
  184.6 17.8 %all-to-all-done.2 = bf16[8,128,1280]{2,1,0:T(8,128)(2,1)S(1)} async-done(((bf16[8,128,1280]{2,1,0:T(8,128)(2,1)}), bf16[8,128,1280]{2,1,0:T(8,128)(2,1)S(1)}, u32[]{:S(2)}, u32[]{:S(2)}) %all-to-all-start.2) | async-done | bytes 2621472 | tf_op jit(solution)/shard_map/all_to_all | solution.py:91
  202.4 1.5 copy-done
  203.9 4.6 %all-to-all-start.3 = ((bf16[8,128,1280]{2,1,0:T(8,128)(2,1)}), bf16[8,128,1280]{2,1,0:T(8,128)(2,1)}, u32[]{:S(2)}, u32[]{:S(2)}) async-start(bf16[8,128,1280]{2,1,0:T(8,128)(2,1)} %bitcast.17), calls=%async_computation.3 | async-start | bytes 5242880 | tf_op jit(solution)/shard_map/all_to_all | solution.py:91
  208.5 6.8 %fusion.6 = f32[512,2048]{1,0:T(8,128)S(1)} fusion(f32[512,2048]{1,0:T(8,128)} %fusion, bf16[2560,2048]{1,0:T(8,128)(2,1)} %all-gather.5.cloned.1.call-done, bf16[128,1280]{1,0:T(8,128)(2,1)} %copy-done.8, bf16[128,1280]{1,0:T(8,128)(2,1)S(1)} %copy-done.7, bf16[128,1280]{1,0:T(8,128)(2,1)} %copy-done.9, bf16[128,1280]{1,0:T(8,128)(2,1)S(1)} %get-tuple-element.17), kind=kOutput, calls=%fused_computation.13 | convolution fusion | flops 2690646016 | bytes 14942208 | tf_op jit(solution)/shard_map/dot_general | solution.py:12
  216.0 3.5 %fusion.13 = f32[512,1280]{1,0:T(8,128)S(1)} fusion(bf16[512,1024]{1,0:T(8,128)(2,1)S(1)} %fusion.31, bf16[1024,2560]{0,1:T(8,128)(2,1)} %all-gather.7.cloned.1.call-done), kind=kOutput, calls=%fused_computation.18 | convolution fusion | flops 1342177280 | bytes 6291456 | tf_op jit(solution)/shard_map/dot_general | solution.py:12
  219.5 1.7 fusion.10
  221.3 2.9 collective-permute-start.12
  224.2 1.4 collective-permute-start.15
  225.6 3.0 %fusion.11 = f32[512,1280]{1,0:T(8,128)} fusion(bf16[512,1024]{1,0:T(8,128)(2,1)S(1)} %fusion.31, bf16[1024,2560]{0,1:T(8,128)(2,1)S(1)} %bitcast.61), kind=kOutput, calls=%fused_computation.16 | convolution fusion | flops 1342177280 | bytes 6291456 | tf_op jit(solution)/shard_map/dot_general | solution.py:12
  228.7 11.9 %all-to-all-done.3 = bf16[8,128,1280]{2,1,0:T(8,128)(2,1)} async-done(((bf16[8,128,1280]{2,1,0:T(8,128)(2,1)}), bf16[8,128,1280]{2,1,0:T(8,128)(2,1)}, u32[]{:S(2)}, u32[]{:S(2)}) %all-to-all-start.3) | async-done | bytes 2621472 | tf_op jit(solution)/shard_map/all_to_all | solution.py:91
  240.5 4.1 %fusion.9 = bf16[512,1280]{1,0:T(8,128)(2,1)S(1)} fusion(f32[512,1280]{1,0:T(8,128)} %fusion.11, bf16[1024,1280]{1,0:T(8,128)(2,1)} %bitcast.18, f32[512]{0:T(512)S(1)} %bitcast.54, s32[512]{0:T(512)S(1)} %multiply_add_fusion), kind=kOutput, calls=%fused_computation.14 | convolution fusion | flops 1344667648 | bytes 6557696 | tf_op jit(solution)/shard_map/dot_general | solution.py:12
  244.7 2.9 collective-permute-start.18
  249.5 1.3 collective-permute-start.13
  251.5 4.2 %collective-permute-done.18 = bf16[128,1280]{1,0:T(8,128)(2,1)S(1)} collective-permute-done((bf16[128,1280]{1,0:T(8,128)(2,1)S(1)}, bf16[128,1280]{1,0:T(8,128)(2,1)S(1)}, u32[]{:S(2)}, u32[]{:S(2)}) %collective-permute-start.18) | collective-permute-done | bytes 327712 | tf_op jit(solution)/shard_map/ppermute | solution.py:37
  255.9 4.4 %collective-permute-start.19 = (bf16[128,1280]{1,0:T(8,128)(2,1)S(1)}, bf16[128,1280]{1,0:T(8,128)(2,1)S(1)}, u32[]{:S(2)}, u32[]{:S(2)}) collective-permute-start(bf16[128,1280]{1,0:T(8,128)(2,1)S(1)} %get-tuple-element.13), channel_id=1, source_target_pairs={{0,1},{1,2},{4,5},{5,6},{8,9},{9,10},{12,13},{13,14},{16,17},{17,1... | collective-permute-start | bytes 983048 | tf_op jit(solution)/shard_map/ppermute | solution.py:37
  261.0 1.8 collective-permute-done.13
  262.9 4.4 %collective-permute-start.14 = (bf16[128,1280]{1,0:T(8,128)(2,1)S(1)}, bf16[128,1280]{1,0:T(8,128)(2,1)S(1)}, u32[]{:S(2)}, u32[]{:S(2)}) collective-permute-start(bf16[128,1280]{1,0:T(8,128)(2,1)S(1)} %get-tuple-element.5), channel_id=1, source_target_pairs={{0,1},{1,2},{2,3},{4,5},{5,6},{6,7},{8,9},{9,10},{10,11},{12,13},{... | collective-permute-start | bytes 983048 | tf_op jit(solution)/shard_map/ppermute | solution.py:37
  267.3 1.3 collective-permute-start.17
  270.0 4.8 %collective-permute-start.20 = (bf16[128,1280]{1,0:T(8,128)(2,1)S(1)}, bf16[128,1280]{1,0:T(8,128)(2,1)S(1)}, u32[]{:S(2)}, u32[]{:S(2)}) collective-permute-start(bf16[128,1280]{1,0:T(8,128)(2,1)S(1)} %get-tuple-element.11), channel_id=1, source_target_pairs={{0,1},{1,2},{2,3},{4,5},{5,6},{6,7},{8,9},{9,10},{10,11},{12,13},{... | collective-permute-start | bytes 983048 | tf_op jit(solution)/shard_map/ppermute | solution.py:37
  274.8 1.3 collective-permute-start.23
  276.1 2.1 collective-permute-done.17
  279.5 4.2 %collective-permute-done.23 = bf16[128,1280]{1,0:T(8,128)(2,1)S(1)} collective-permute-done((bf16[128,1280]{1,0:T(8,128)(2,1)S(1)}, bf16[128,1280]{1,0:T(8,128)(2,1)S(1)}, u32[]{:S(2)}, u32[]{:S(2)}) %collective-permute-start.23) | collective-permute-done | bytes 327712 | tf_op jit(solution)/shard_map/ppermute | solution.py:38
  (97 shorter events, 16.4 us)
Async XLA Ops:
  6.5 2.6 copy-start.2
  6.5 16.1 %copy-start.11 = (s32[128,1]{0,1:T(1,128)S(1)}, s32[128,1]{0,1:T(1,128)}, u32[]{:S(2)}) copy-start(s32[128,1]{0,1:T(1,128)} %param.10) | copy-start | bytes 1540
  6.5 16.1 %copy-start.10 = (f32[128]{0:T(128)S(1)}, f32[128]{0:T(128)}, u32[]{:S(2)}) copy-start(f32[128]{0:T(128)} %param.11) | copy-start | bytes 1540
  6.5 170.5 %all-gather.5.cloned.1.call-start = ((), (), s32[]{:S(2)}) async-start(), calls=%async_computation.4 | async-start | bytes 11796480 | tf_op jit(solution)/shard_map/all_gather | solution.py:57
  9.2 26.5 %collective-permute-start.6 = (bf16[128,1280]{1,0:T(8,128)(2,1)S(1)}, bf16[128,1280]{1,0:T(8,128)(2,1)S(1)}, u32[]{:S(2)}, u32[]{:S(2)}) collective-permute-start(bf16[128,1280]{1,0:T(8,128)(2,1)S(1)} %get-tuple-element.18), channel_id=1, source_target_pairs={{0,1},{1,2},{2,3},{4,5},{5,6},{6,7},{8,9},{9,10},{10,11},{12,13},{... | collective-permute-start | bytes 983048 | tf_op jit(solution)/shard_map/ppermute | solution.py:18
  14.2 22.2 %collective-permute-start.7 = (bf16[128,1280]{1,0:T(8,128)(2,1)S(1)}, bf16[128,1280]{1,0:T(8,128)(2,1)S(1)}, u32[]{:S(2)}, u32[]{:S(2)}) collective-permute-start(bf16[128,1280]{1,0:T(8,128)(2,1)S(1)} %get-tuple-element.18), channel_id=1, source_target_pairs={{1,0},{2,1},{3,2},{5,4},{6,5},{7,6},{9,8},{10,9},{11,10},{13,12},{... | collective-permute-start | bytes 983048 | tf_op jit(solution)/shard_map/ppermute | solution.py:19
  15.5 48.4 %collective-permute-start.1 = (bf16[128,1280]{1,0:T(8,128)(2,1)S(1)}, bf16[128,1280]{1,0:T(8,128)(2,1)}, u32[]{:S(2)}, u32[]{:S(2)}) collective-permute-start(bf16[128,1280]{1,0:T(8,128)(2,1)S(1)} %get-tuple-element.17), channel_id=1, source_target_pairs={{1,0},{2,1},{3,2},{5,4},{6,5},{7,6},{9,8},{10,9},{11,10},{13,12},{... | collective-permute-start | bytes 983048 | tf_op jit(solution)/shard_map/ppermute | solution.py:19
  16.8 46.4 %collective-permute-start = (bf16[128,1280]{1,0:T(8,128)(2,1)S(1)}, bf16[128,1280]{1,0:T(8,128)(2,1)}, u32[]{:S(2)}, u32[]{:S(2)}) collective-permute-start(bf16[128,1280]{1,0:T(8,128)(2,1)S(1)} %get-tuple-element.17), channel_id=1, source_target_pairs={{0,1},{1,2},{2,3},{4,5},{5,6},{6,7},{8,9},{9,10},{10,11},{12,13},{... | collective-permute-start | bytes 983048 | tf_op jit(solution)/shard_map/ppermute | solution.py:18
  35.6 2.3 collective-permute-start.10
  36.3 10.9 %collective-permute-start.8 = (bf16[128,1280]{1,0:T(8,128)(2,1)S(1)}, bf16[128,1280]{1,0:T(8,128)(2,1)S(1)}, u32[]{:S(2)}, u32[]{:S(2)}) collective-permute-start(bf16[128,1280]{1,0:T(8,128)(2,1)S(1)} %collective-permute-done.7), channel_id=1, source_target_pairs={{1,0},{2,1},{5,4},{6,5},{9,8},{10,9},{13,12},{14,13},{17,16},{18,1... | collective-permute-start | bytes 983048 | tf_op jit(solution)/shard_map/ppermute | solution.py:19
  37.9 10.7 %collective-permute-start.11 = (bf16[128,1280]{1,0:T(8,128)(2,1)S(1)}, bf16[128,1280]{1,0:T(8,128)(2,1)S(1)}, u32[]{:S(2)}, u32[]{:S(2)}) collective-permute-start(bf16[128,1280]{1,0:T(8,128)(2,1)S(1)} %collective-permute-done.10), channel_id=1, source_target_pairs={{2,3},{6,7},{10,11},{14,15},{18,19},{22,23},{26,27},{30,31}} | collective-permute-start | bytes 983048 | tf_op jit(solution)/shard_map/ppermute | solution.py:18
  47.2 9.0 %collective-permute-start.9 = (bf16[128,1280]{1,0:T(8,128)(2,1)S(1)}, bf16[128,1280]{1,0:T(8,128)(2,1)S(1)}, u32[]{:S(2)}, u32[]{:S(2)}) collective-permute-start(bf16[128,1280]{1,0:T(8,128)(2,1)S(1)} %collective-permute-done.8), channel_id=1, source_target_pairs={{1,0},{5,4},{9,8},{13,12},{17,16},{21,20},{25,24},{29,28}} | collective-permute-start | bytes 983048 | tf_op jit(solution)/shard_map/ppermute | solution.py:19
  48.6 10.9 %copy-start.3 = (bf16[128,1280]{1,0:T(8,128)(2,1)}, bf16[128,1280]{1,0:T(8,128)(2,1)S(1)}, u32[]{:S(2)}) copy-start(bf16[128,1280]{1,0:T(8,128)(2,1)S(1)} %broadcast_select_fusion.2) | copy-start | bytes 983044
  48.6 10.8 %copy-start.4 = (bf16[128,1280]{1,0:T(8,128)(2,1)}, bf16[128,1280]{1,0:T(8,128)(2,1)S(1)}, u32[]{:S(2)}) copy-start(bf16[128,1280]{1,0:T(8,128)(2,1)S(1)} %broadcast_select_fusion) | copy-start | bytes 983044
  56.2 3.2 %copy-start.5 = (bf16[128,1280]{1,0:T(8,128)(2,1)}, bf16[128,1280]{1,0:T(8,128)(2,1)S(1)}, u32[]{:S(2)}) copy-start(bf16[128,1280]{1,0:T(8,128)(2,1)S(1)} %broadcast_select_fusion.4) | copy-start | bytes 983044
  59.4 42.6 %all-to-all-start.1 = ((bf16[8,128,1280]{2,1,0:T(8,128)(2,1)}), bf16[8,128,1280]{2,1,0:T(8,128)(2,1)S(1)}, u32[]{:S(2)}, u32[]{:S(2)}) async-start(bf16[8,128,1280]{2,1,0:T(8,128)(2,1)} %bitcast.47), calls=%async_computation.1 | async-start | bytes 5242880 | tf_op jit(solution)/shard_map/all_to_all | solution.py:75
  63.2 2.0 collective-permute-start.4
  63.9 12.2 %collective-permute-start.2 = (bf16[128,1280]{1,0:T(8,128)(2,1)}, bf16[128,1280]{1,0:T(8,128)(2,1)S(1)}, u32[]{:S(2)}, u32[]{:S(2)}) collective-permute-start(bf16[128,1280]{1,0:T(8,128)(2,1)} %collective-permute-done.1), channel_id=1, source_target_pairs={{1,0},{2,1},{5,4},{6,5},{9,8},{10,9},{13,12},{14,13},{17,16},{18,1... | collective-permute-start | bytes 983048 | tf_op jit(solution)/shard_map/ppermute | solution.py:19
  65.2 12.2 %collective-permute-start.5 = (bf16[128,1280]{1,0:T(8,128)(2,1)S(1)}, bf16[128,1280]{1,0:T(8,128)(2,1)S(1)}, u32[]{:S(2)}, u32[]{:S(2)}) collective-permute-start(bf16[128,1280]{1,0:T(8,128)(2,1)S(1)} %collective-permute-done.4), channel_id=1, source_target_pairs={{2,3},{6,7},{10,11},{14,15},{18,19},{22,23},{26,27},{30,31}} | collective-permute-start | bytes 983048 | tf_op jit(solution)/shard_map/ppermute | solution.py:18
  76.1 11.2 %collective-permute-start.3 = (bf16[128,1280]{1,0:T(8,128)(2,1)S(1)}, bf16[128,1280]{1,0:T(8,128)(2,1)S(1)}, u32[]{:S(2)}, u32[]{:S(2)}) collective-permute-start(bf16[128,1280]{1,0:T(8,128)(2,1)S(1)} %collective-permute-done.2), channel_id=1, source_target_pairs={{1,0},{5,4},{9,8},{13,12},{17,16},{21,20},{25,24},{29,28}} | collective-permute-start | bytes 983048 | tf_op jit(solution)/shard_map/ppermute | solution.py:19
  77.4 10.0 %copy-start.6 = (bf16[128,1280]{1,0:T(8,128)(2,1)}, bf16[128,1280]{1,0:T(8,128)(2,1)S(1)}, u32[]{:S(2)}) copy-start(bf16[128,1280]{1,0:T(8,128)(2,1)S(1)} %broadcast_select_fusion.3) | copy-start | bytes 983044
  78.6 8.8 %copy-start.8 = (bf16[128,1280]{1,0:T(8,128)(2,1)}, bf16[128,1280]{1,0:T(8,128)(2,1)S(1)}, u32[]{:S(2)}) copy-start(bf16[128,1280]{1,0:T(8,128)(2,1)S(1)} %broadcast_select_fusion.1) | copy-start | bytes 983044
  102.1 43.7 %all-to-all-start = ((bf16[8,128,1280]{2,1,0:T(8,128)(2,1)}), bf16[8,128,1280]{2,1,0:T(8,128)(2,1)}, u32[]{:S(2)}, u32[]{:S(2)}) async-start(bf16[8,128,1280]{2,1,0:T(8,128)(2,1)} %bitcast.49), calls=%async_computation | async-start | bytes 5242880 | tf_op jit(solution)/shard_map/all_to_all | solution.py:75
  106.5 109.6 %all-gather.7.cloned.1.call-start = ((), (), s32[]{:S(2)}) async-start(), calls=%async_computation.5 | async-start | bytes 5898240 | tf_op jit(solution)/shard_map/all_gather | solution.py:86
  145.7 10.9 %slice-start = ((s8[5242880]{0:T(1024)(128)(4,1)}), s8[4194304]{0:T(1024)(128)(4,1)S(1)}, s32[]{:S(2)}) async-start(s8[5242880]{0:T(1024)(128)(4,1)} %bitcast.56), calls=%async_computation.6 | async-start | bytes 8388608
  151.8 4.8 %slice-start.1 = ((s8[5242880]{0:T(1024)(128)(4,1)}), s8[1048576]{0:T(1024)(128)(4,1)S(1)}, s32[]{:S(2)}) async-start(s8[5242880]{0:T(1024)(128)(4,1)} %bitcast.56), calls=%async_computation.7 | async-start | bytes 2097152
  151.8 4.8 %copy-start.12 = (f32[1024,1024]{1,0:T(8,128)S(1)}, f32[1024,1024]{1,0:T(8,128)}, u32[]{:S(2)}) copy-start(f32[1024,1024]{1,0:T(8,128)} %fusion.17) | copy-start | bytes 12582916
  151.8 10.6 %slice-start.2 = ((s8[5242880]{0:T(1024)(128)(4,1)}), s8[4194304]{0:T(1024)(128)(4,1)S(1)}, s32[]{:S(2)}) async-start(s8[5242880]{0:T(1024)(128)(4,1)} %bitcast.58), calls=%async_computation.8 | async-start | bytes 8388608
  156.6 5.7 %slice-start.3 = ((s8[5242880]{0:T(1024)(128)(4,1)}), s8[1048576]{0:T(1024)(128)(4,1)S(1)}, s32[]{:S(2)}) async-start(s8[5242880]{0:T(1024)(128)(4,1)} %bitcast.58), calls=%async_computation.9 | async-start | bytes 2097152
  162.4 4.2 %copy-start.13 = (bf16[1024,1024]{1,0:T(8,128)(2,1)}, bf16[1024,1024]{1,0:T(8,128)(2,1)S(1)}, u32[]{:S(2)}) copy-start(bf16[1024,1024]{1,0:T(8,128)(2,1)S(1)} %multiply_convert_fusion) | copy-start | bytes 6291460
  166.6 35.8 %all-to-all-start.2 = ((bf16[8,128,1280]{2,1,0:T(8,128)(2,1)}), bf16[8,128,1280]{2,1,0:T(8,128)(2,1)S(1)}, u32[]{:S(2)}, u32[]{:S(2)}) async-start(bf16[8,128,1280]{2,1,0:T(8,128)(2,1)} %bitcast.50), calls=%async_computation.2 | async-start | bytes 5242880 | tf_op jit(solution)/shard_map/all_to_all | solution.py:91
  202.4 6.1 %copy-start.7 = (bf16[128,1280]{1,0:T(8,128)(2,1)S(1)}, bf16[128,1280]{1,0:T(8,128)(2,1)}, u32[]{:S(2)}) copy-start(bf16[128,1280]{1,0:T(8,128)(2,1)} %copy-done.6) | copy-start | bytes 983044
  203.9 36.7 %all-to-all-start.3 = ((bf16[8,128,1280]{2,1,0:T(8,128)(2,1)}), bf16[8,128,1280]{2,1,0:T(8,128)(2,1)}, u32[]{:S(2)}, u32[]{:S(2)}) async-start(bf16[8,128,1280]{2,1,0:T(8,128)(2,1)} %bitcast.17), calls=%async_computation.3 | async-start | bytes 5242880 | tf_op jit(solution)/shard_map/all_to_all | solution.py:91
  216.0 3.5 %copy-start.1 = (bf16[8,128,1280]{2,1,0:T(8,128)(2,1)S(1)}, bf16[8,128,1280]{2,1,0:T(8,128)(2,1)}, u32[]{:S(2)}) copy-start(bf16[8,128,1280]{2,1,0:T(8,128)(2,1)} %copy-done) | copy-start | bytes 7864324
  216.0 9.6 %slice-start.4 = ((s8[5242880]{0:T(1024)(128)(4,1)}), s8[4194304]{0:T(1024)(128)(4,1)S(1)}, s32[]{:S(2)}) async-start(s8[5242880]{0:T(1024)(128)(4,1)} %bitcast.60), calls=%async_computation.10 | async-start | bytes 8388608
  219.5 6.1 %slice-start.5 = ((s8[5242880]{0:T(1024)(128)(4,1)}), s8[1048576]{0:T(1024)(128)(4,1)S(1)}, s32[]{:S(2)}) async-start(s8[5242880]{0:T(1024)(128)(4,1)} %bitcast.60), calls=%async_computation.11 | async-start | bytes 2097152
  221.3 27.1 %collective-permute-start.12 = (bf16[128,1280]{1,0:T(8,128)(2,1)S(1)}, bf16[128,1280]{1,0:T(8,128)(2,1)S(1)}, u32[]{:S(2)}, u32[]{:S(2)}) collective-permute-start(bf16[128,1280]{1,0:T(8,128)(2,1)S(1)} %get-tuple-element.9), channel_id=1, source_target_pairs={{0,1},{4,5},{8,9},{12,13},{16,17},{20,21},{24,25},{28,29}} | collective-permute-start | bytes 983048 | tf_op jit(solution)/shard_map/ppermute | solution.py:37
  224.2 24.2 %collective-permute-start.15 = (bf16[128,1280]{1,0:T(8,128)(2,1)S(1)}, bf16[128,1280]{1,0:T(8,128)(2,1)}, u32[]{:S(2)}, u32[]{:S(2)}) collective-permute-start(bf16[128,1280]{1,0:T(8,128)(2,1)S(1)} %get-tuple-element.10), channel_id=1, source_target_pairs={{3,2},{7,6},{11,10},{15,14},{19,18},{23,22},{27,26},{31,30}} | collective-permute-start | bytes 983048 | tf_op jit(solution)/shard_map/ppermute | solution.py:38
  244.7 11.0 %collective-permute-start.18 = (bf16[128,1280]{1,0:T(8,128)(2,1)S(1)}, bf16[128,1280]{1,0:T(8,128)(2,1)S(1)}, u32[]{:S(2)}, u32[]{:S(2)}) collective-permute-start(bf16[128,1280]{1,0:T(8,128)(2,1)S(1)} %get-tuple-element.15), channel_id=1, source_target_pairs={{0,1},{4,5},{8,9},{12,13},{16,17},{20,21},{24,25},{28,29}} | collective-permute-start | bytes 983048 | tf_op jit(solution)/shard_map/ppermute | solution.py:37
  247.7 8.1 %collective-permute-start.21 = (bf16[128,1280]{1,0:T(8,128)(2,1)S(1)}, bf16[128,1280]{1,0:T(8,128)(2,1)S(1)}, u32[]{:S(2)}, u32[]{:S(2)}) collective-permute-start(bf16[128,1280]{1,0:T(8,128)(2,1)S(1)} %get-tuple-element.16), channel_id=1, source_target_pairs={{3,2},{7,6},{11,10},{15,14},{19,18},{23,22},{27,26},{31,30}} | collective-permute-start | bytes 983048 | tf_op jit(solution)/shard_map/ppermute | solution.py:38
  249.5 13.3 %collective-permute-start.13 = (bf16[128,1280]{1,0:T(8,128)(2,1)S(1)}, bf16[128,1280]{1,0:T(8,128)(2,1)S(1)}, u32[]{:S(2)}, u32[]{:S(2)}) collective-permute-start(bf16[128,1280]{1,0:T(8,128)(2,1)S(1)} %get-tuple-element.7), channel_id=1, source_target_pairs={{0,1},{1,2},{4,5},{5,6},{8,9},{9,10},{12,13},{13,14},{16,17},{17,1... | collective-permute-start | bytes 983048 | tf_op jit(solution)/shard_map/ppermute | solution.py:37
  250.8 12.0 %collective-permute-start.16 = (bf16[128,1280]{1,0:T(8,128)(2,1)S(1)}, bf16[128,1280]{1,0:T(8,128)(2,1)S(1)}, u32[]{:S(2)}, u32[]{:S(2)}) collective-permute-start(bf16[128,1280]{1,0:T(8,128)(2,1)S(1)} %get-tuple-element.8), channel_id=1, source_target_pairs={{2,1},{3,2},{6,5},{7,6},{10,9},{11,10},{14,13},{15,14},{18,17},{19... | collective-permute-start | bytes 983048 | tf_op jit(solution)/shard_map/ppermute | solution.py:38
  255.9 13.9 %collective-permute-start.19 = (bf16[128,1280]{1,0:T(8,128)(2,1)S(1)}, bf16[128,1280]{1,0:T(8,128)(2,1)S(1)}, u32[]{:S(2)}, u32[]{:S(2)}) collective-permute-start(bf16[128,1280]{1,0:T(8,128)(2,1)S(1)} %get-tuple-element.13), channel_id=1, source_target_pairs={{0,1},{1,2},{4,5},{5,6},{8,9},{9,10},{12,13},{13,14},{16,17},{17,1... | collective-permute-start | bytes 983048 | tf_op jit(solution)/shard_map/ppermute | solution.py:37
  260.3 9.5 %collective-permute-start.22 = (bf16[128,1280]{1,0:T(8,128)(2,1)S(1)}, bf16[128,1280]{1,0:T(8,128)(2,1)S(1)}, u32[]{:S(2)}, u32[]{:S(2)}) collective-permute-start(bf16[128,1280]{1,0:T(8,128)(2,1)S(1)} %get-tuple-element.14), channel_id=1, source_target_pairs={{2,1},{3,2},{6,5},{7,6},{10,9},{11,10},{14,13},{15,14},{18,17},{19... | collective-permute-start | bytes 983048 | tf_op jit(solution)/shard_map/ppermute | solution.py:38
  262.9 13.2 %collective-permute-start.14 = (bf16[128,1280]{1,0:T(8,128)(2,1)S(1)}, bf16[128,1280]{1,0:T(8,128)(2,1)S(1)}, u32[]{:S(2)}, u32[]{:S(2)}) collective-permute-start(bf16[128,1280]{1,0:T(8,128)(2,1)S(1)} %get-tuple-element.5), channel_id=1, source_target_pairs={{0,1},{1,2},{2,3},{4,5},{5,6},{6,7},{8,9},{9,10},{10,11},{12,13},{... | collective-permute-start | bytes 983048 | tf_op jit(solution)/shard_map/ppermute | solution.py:37
  267.3 10.9 %collective-permute-start.17 = (bf16[128,1280]{1,0:T(8,128)(2,1)S(1)}, bf16[128,1280]{1,0:T(8,128)(2,1)S(1)}, u32[]{:S(2)}, u32[]{:S(2)}) collective-permute-start(bf16[128,1280]{1,0:T(8,128)(2,1)S(1)} %get-tuple-element.6), channel_id=1, source_target_pairs={{1,0},{2,1},{3,2},{5,4},{6,5},{7,6},{9,8},{10,9},{11,10},{13,12},{... | collective-permute-start | bytes 983048 | tf_op jit(solution)/shard_map/ppermute | solution.py:38
  270.0 9.6 %collective-permute-start.20 = (bf16[128,1280]{1,0:T(8,128)(2,1)S(1)}, bf16[128,1280]{1,0:T(8,128)(2,1)S(1)}, u32[]{:S(2)}, u32[]{:S(2)}) collective-permute-start(bf16[128,1280]{1,0:T(8,128)(2,1)S(1)} %get-tuple-element.11), channel_id=1, source_target_pairs={{0,1},{1,2},{2,3},{4,5},{5,6},{6,7},{8,9},{9,10},{10,11},{12,13},{... | collective-permute-start | bytes 983048 | tf_op jit(solution)/shard_map/ppermute | solution.py:37
  274.8 9.0 %collective-permute-start.23 = (bf16[128,1280]{1,0:T(8,128)(2,1)S(1)}, bf16[128,1280]{1,0:T(8,128)(2,1)S(1)}, u32[]{:S(2)}, u32[]{:S(2)}) collective-permute-start(bf16[128,1280]{1,0:T(8,128)(2,1)S(1)} %get-tuple-element.12), channel_id=1, source_target_pairs={{1,0},{2,1},{3,2},{5,4},{6,5},{7,6},{9,8},{10,9},{11,10},{13,12},{... | collective-permute-start | bytes 983048 | tf_op jit(solution)/shard_map/ppermute | solution.py:38
  (2 other events, 2.2 us)
Sparse Core Ops, SparseCore 0:
  9.2 72.5 all-gather.4
  109.2 56.4 all-gather.6
